TPU v7x, 32 devices: a whole 2x2x4 slice. The times are simulated.
32 devices in a mesh: role: 2 (over core), seq: 4 (over z), tp: 4 (over y, x).
Axes of the slice: x: 2, y: 2, z: 4, core: 2. Of those that a mesh axis runs over, the one named last changes fastest.
Arguments:
- merger_hidden: bfloat16 [512, 5120], P(('role', 'seq'), 'tp'), may hold values from -6 to 6
- merger_out: bfloat16 [5120, 8192], P('tp', ('role', 'seq')), may hold values from -0.078125 to 0.078125
- row_position: int32 [512], P(('role', 'seq')), may hold values from -1 to 2047, as said below
- prompt_embeds: bfloat16 [2048, 8192], P(('role', 'seq'), 'tp'), may hold values from -300 to 300
- norm_gain: bfloat16 [8192], P('tp'), may hold values from 0.099609375 to 1.8984375
- query_weight: bfloat16 [8192, 4096], P(None, 'tp'), may hold values from -2.762136 to 2.762136
- key_weight: bfloat16 [8192, 512], P(None, 'tp'), may hold values from -0.06629126 to 0.06629126
- value_weight: bfloat16 [8192, 512], P(None, 'tp'), may hold values from -0.0625 to 0.0625
Outputs:
- stream: bfloat16 [2048, 8192], P(('role', 'seq'), 'tp')
- context: bfloat16 [2048, 4096], P(('role', 'seq'), 'tp')
Inputs may be any that keep to these rules, and one draw needn't show every extreme that they name: `row_position`: the live slots of each device's 64 come first and hold distinct prompt positions, distinct over all devices; the other slots hold -1. Of one device's slots at most 16 hold positions of one owner's block (positions j * 256 to (j + 1) * 256 - 1); every device has 16 or more live slots.
All inputs are finite; a program needn't handle non-finite values.
Results may differ from a plain program's by a relative error of at most 0.012.
The roundings to bfloat16 on the way count: a program that leaves them out, or rounds other values in their place, can miss the bound.
Values may be sent and summed in bfloat16 or wider, within the bound.
No kernel may reach another device: no remote copies, remote signals or barrier semaphores. Data moves between devices by JAX's collectives and lax.ppermute only.
A program may use at most 192 MiB of HBM per device.

v0:
```python
import math
import jax
import jax.numpy as jnp
from jax import lax
from jax.sharding import PartitionSpec as P

HEAD_DIM = 128


def rotate(vectors, positions):
    half_dim = vectors.shape[-1] // 2
    frequency = 1000000.0 ** (-jnp.arange(half_dim, dtype=jnp.float32) / half_dim)
    angles = positions.astype(jnp.float32)[:, None, None] * frequency[None, None, :]
    cosine = jnp.cos(angles)
    sine_part = jnp.sin(angles)
    lower_half = vectors[..., :half_dim]
    upper_half = vectors[..., half_dim:]
    return jnp.concatenate(
        [
            lower_half * cosine - upper_half * sine_part,
            upper_half * cosine + lower_half * sine_part,
        ],
        axis=-1,
    )


def sum_hidden(partial_value):
    return lax.psum_scatter(partial_value, "tp", scatter_dimension=1, tiled=True).astype(
        jnp.bfloat16
    )


def project_strips(merger_hidden, merger_out):
    return jnp.dot(
        lax.all_gather(merger_hidden, ("role", "seq"), axis=0, tiled=True),
        merger_out,
        preferred_element_type=jnp.float32,
    )


def body(
    merger_hidden,
    merger_out,
    row_position,
    prompt_embeds,
    norm_gain,
    query_weight,
    key_weight,
    value_weight,
):
    groups = lax.axis_size("role") * lax.axis_size("seq")
    device_rank = lax.axis_index(("role", "seq"))
    row_count = merger_hidden.shape[0]
    tok_count = prompt_embeds.shape[0]
    columns = prompt_embeds.shape[1]
    model_width = columns * lax.axis_size("tp")
    capacity = 2 * row_count // groups
    strips = project_strips(merger_hidden, merger_out)
    partial_value = lax.all_to_all(strips, ("role", "seq"), split_axis=0, concat_axis=1, tiled=True)
    embeds = sum_hidden(partial_value)
    owners = jnp.where(row_position >= 0, row_position // tok_count, groups)
    onehot = (owners[:, None] == jnp.arange(groups, dtype=jnp.int32)[None, :]).astype(jnp.int32)
    earlier = jnp.sum((jnp.cumsum(onehot, axis=0) - onehot) * onehot, axis=1)
    buffer_slot = jnp.where(owners < groups, owners * capacity + earlier, groups * capacity)
    source = (
        jnp.full((groups * capacity,), row_count, jnp.int32)
        .at[buffer_slot]
        .set(jnp.arange(row_count, dtype=jnp.int32), mode="drop")
    )
    padded = jnp.concatenate([embeds, jnp.zeros((1, columns), jnp.bfloat16)], axis=0)
    outgoing = padded[source].reshape(groups, capacity, columns)
    outgoing_pos = jnp.concatenate([row_position, jnp.full((1,), -1, jnp.int32)])[source].reshape(
        groups, capacity
    )
    arrived, arrived_pos = (
        lax.all_to_all(outgoing, ("role", "seq"), split_axis=0, concat_axis=0, tiled=True),
        lax.all_to_all(outgoing_pos, ("role", "seq"), split_axis=0, concat_axis=0, tiled=True),
    )
    arrived_pos = arrived_pos.reshape(-1)
    local_row = jnp.where(arrived_pos >= 0, arrived_pos - device_rank * tok_count, tok_count)
    stream = prompt_embeds.at[local_row].set(arrived.reshape(-1, columns), mode="drop")
    widened = stream.astype(jnp.float32)
    squares = lax.psum(jnp.sum(widened * widened, axis=1), "tp")
    inverse = lax.rsqrt(squares / model_width + 1e-06)[:, None]
    normed = (widened * inverse * norm_gain.astype(jnp.float32)[None, :]).astype(jnp.bfloat16)
    tables = (query_weight, key_weight, value_weight)
    shard_piece = lax.all_gather(normed, "tp", axis=1, tiled=True)
    query_sum, key_sum, value_sum = tuple(
        (jnp.dot(shard_piece, table, preferred_element_type=jnp.float32) for table in tables)
    )
    local_heads = query_weight.shape[1] // HEAD_DIM
    local_kv = key_weight.shape[1] // HEAD_DIM
    group_size = local_heads // local_kv
    positions = device_rank * tok_count + jnp.arange(tok_count, dtype=jnp.int32)
    queries = rotate(query_sum.reshape(tok_count, local_heads, HEAD_DIM), positions).astype(
        jnp.bfloat16
    )
    queries = queries.reshape(tok_count, local_kv, group_size, HEAD_DIM)
    key_rows = rotate(key_sum.reshape(tok_count, local_kv, HEAD_DIM), positions).astype(
        jnp.bfloat16
    )
    value_rows = value_sum.astype(jnp.bfloat16).reshape(tok_count, local_kv, HEAD_DIM)
    score_scale = 1.0 / math.sqrt(HEAD_DIM)
    running_max = jnp.full((local_kv, group_size, tok_count), -1e30, jnp.float32)
    key_piece = lax.all_gather(key_rows, ("role", "seq"), axis=0, tiled=True)
    value_piece = lax.all_gather(value_rows, ("role", "seq"), axis=0, tiled=True)
    scores = (
        jnp.einsum("qhgd,khd->hgqk", queries, key_piece, preferred_element_type=jnp.float32)
        * score_scale
    )
    key_pos = jnp.arange(key_piece.shape[0], dtype=jnp.int32)
    visible = key_pos[None, :] <= positions[:, None]
    scores = jnp.where(visible, scores, -jnp.inf)
    next_max = jnp.maximum(running_max, jnp.max(scores, axis=3))
    probability = jnp.where(visible, jnp.exp(scores - next_max[..., None]), 0.0)
    running_sum = jnp.sum(probability, axis=3)
    running_out = jnp.einsum(
        "hgqk,khd->hgqd",
        probability.astype(jnp.bfloat16),
        value_piece,
        preferred_element_type=jnp.float32,
    )
    running_max, running_sum, running_out = (next_max, running_sum, running_out)
    context = running_out / running_sum[..., None]
    context = (
        jnp.transpose(context, (2, 0, 1, 3))
        .reshape(tok_count, local_heads * HEAD_DIM)
        .astype(jnp.bfloat16)
    )
    return (stream, context)


def solution(mesh):
    in_specs = (
        P(("role", "seq"), "tp"),
        P("tp", ("role", "seq")),
        P(("role", "seq")),
        P(("role", "seq"), "tp"),
        P("tp"),
        P(None, "tp"),
        P(None, "tp"),
        P(None, "tp"),
    )
    out_specs = (P(("role", "seq"), "tp"), P(("role", "seq"), "tp"))
    return jax.shard_map(body, mesh=mesh, in_specs=in_specs, out_specs=out_specs, check_vma=False)
```

profile of v0, /device:TPU:0, one launch (start us, length us, event | category | flops | bytes accessed | tf_op | source)
XLA Modules:
  0.0 304.1 jit_solution(15773914192989135023)
XLA Ops:
  7.2 0.0 copy-start
  7.2 0.0 all-gather.4.cloned.1.call-start
  7.2 2.5 copy.45
  9.7 0.0 all-gather.4.cloned.1.call-update
  9.7 0.0 reduce-scatter.2.cloned.1.call-start
  9.8 26.2 %all-gather.4.cloned.1.call-done = bf16[512,1280]{1,0:T(8,128)(2,1)} async-done(((bf16[64,1280]{1,0:T(8,128)(2,1)}), bf16[512,1280]{1,0:T(8,128)(2,1)}) %all-gather.4.cloned.1.call-update) | async-done | bytes 1310736 | tf_op jit(solution)/shard_map/all_gather | solution.py:35
  36.0 2.8 fusion.37
  38.8 51.7 %all_to_all.33 = f32[8,64,1024]{2,1,0:T(8,128)S(1)} all-to-all(f32[8,64,1024]{2,1,0:T(8,128)S(1)} %bitcast.65), channel_id=1, replica_groups=mesh['role'=2,'seq'=4,'tp'=4] {'role','seq'}, dimensions={0} | all-to-all | bytes 4194304 | tf_op jit(solution)/shard_map/all_to_all | solution.py:59
  90.5 1.5 copy.37
  92.0 0.0 reduce-scatter.2.cloned.1.call-update
  92.1 0.0 copy-start.3
  92.1 0.1 fusion.26
  92.2 0.1 reduce_window_sum.11
  92.3 0.2 select_reduce_fusion
  92.5 0.8 scatter_custom_fusion
  93.3 0.1 pad_add_fusion
  93.3 1.2 gather_fusion
  94.6 0.7 all_to_all.23
  95.2 3.3 %all-to-all-start = ((s32[8,1,16]{2,1,0:T(1,128)}), s32[8,1,16]{2,1,0:T(1,128)S(1)}, u32[]{:S(2)}, u32[]{:S(2)}) async-start(s32[8,1,16]{2,1,0:T(1,128)} %bitcast), calls=%async_computation | async-start | bytes 8192 | tf_op jit(solution)/shard_map/all_to_all | solution.py:77
  98.5 27.3 %reduce-scatter.2.cloned.1.call-done = f32[64,2048]{1,0:T(8,128)} async-done(((f32[64,8192]{1,0:T(8,128)}), f32[64,2048]{1,0:T(8,128)}) %reduce-scatter.2.cloned.1.call-update) | async-done | bytes 524304 | tf_op jit(solution)/shard_map/reduce_scatter | solution.py:28
  125.9 1.1 convert_element_type.54
  127.0 1.7 gather_fusion.1
  128.7 4.6 %all-to-all-start.2 = ((bf16[8,16,2048]{2,1,0:T(8,128)(2,1)}), bf16[8,16,2048]{2,1,0:T(8,128)(2,1)S(1)}, u32[]{:S(2)}, u32[]{:S(2)}) async-start(bf16[8,16,2048]{2,1,0:T(8,128)(2,1)} %bitcast.4), calls=%async_computation.3 | async-start | bytes 1048576 | tf_op jit(solution)/shard_map/all_to_all | solution.py:76
  133.3 0.0 all-gather.6.cloned.1.call-start
  133.4 0.1 select_n.56
  133.5 14.6 %all-to-all-done.2 = bf16[8,16,2048]{2,1,0:T(8,128)(2,1)S(1)} async-done(((bf16[8,16,2048]{2,1,0:T(8,128)(2,1)}), bf16[8,16,2048]{2,1,0:T(8,128)(2,1)S(1)}, u32[]{:S(2)}, u32[]{:S(2)}) %all-to-all-start.2) | async-done | bytes 524320 | tf_op jit(solution)/shard_map/all_to_all | solution.py:76
  148.0 3.7 %scatter_fusion = bf16[256,2048]{1,0:T(8,128)(2,1)} fusion(bf16[256,2048]{1,0:T(8,128)(2,1)} %copy.45, s32[128]{0:T(128)S(1)} %fusion.28, bf16[128,2048]{1,0:T(8,128)(2,1)S(1)} %bitcast.64), kind=kCustom, calls=%fused_computation.3 | custom fusion | bytes 1573376 | tf_op jit(solution)/shard_map/scatter | solution.py:81
  151.7 1.5 fusion.7
  153.2 8.9 %psum.7 = f32[256]{0:T(256)S(1)} all-reduce(f32[256]{0:T(256)S(1)} %fusion.7), channel_id=1, replica_groups=mesh['role'=2,'seq'=4,'tp'=4] {'tp'}, use_global_device_ids=true, to_apply=%region_6.7 | all-reduce | flops 256 | bytes 2048 | tf_op jit(solution)/shard_map/psum | solution.py:83
  162.2 2.5 fusion.9
  164.7 0.0 all-gather.6.cloned.1.call-update
  164.7 0.5 multiply_cosine_fusion
  165.3 0.3 iota_compare_fusion
  165.6 49.5 %all-gather.6.cloned.1.call-done = bf16[256,8192]{1,0:T(8,128)(2,1)} async-done(((bf16[256,2048]{1,0:T(8,128)(2,1)}), bf16[256,8192]{1,0:T(8,128)(2,1)}) %all-gather.6.cloned.1.call-update) | async-done | bytes 4194320 | tf_op jit(solution)/shard_map/all_gather | solution.py:87
  215.1 4.5 %convolution_bitcast_fusion.1 = f32[256,1,128]{0,2,1:T(8,128)S(1)} fusion(bf16[256,8192]{1,0:T(8,128)(2,1)} %all-gather.6.cloned.1.call-done, bf16[8192,128]{1,0:T(8,128)(2,1)} %param.14), kind=kOutput, calls=%fused_computation.19 | convolution fusion | flops 536870912 | bytes 6422528 | tf_op jit(solution)/shard_map/dot_general | solution.py:89
  219.6 0.3 fusion.23
  219.9 0.0 copy-start.2
  219.9 8.4 %convolution_bitcast_fusion = f32[32,8,8,128]{3,1,2,0:T(8,128)S(1)} fusion(bf16[256,8192]{1,0:T(8,128)(2,1)S(1)} %copy-done.1, bf16[8192,1024]{1,0:T(8,128)(2,1)} %param.13), kind=kOutput, calls=%fused_computation.18 | convolution fusion | flops 4294967296 | bytes 22020096 | tf_op jit(solution)/shard_map/dot_general | solution.py:89
  228.4 0.2 copy.38
  228.6 26.5 %all_gather.14 = bf16[2048,1,128]{0,2,1:T(8,128)(2,1)S(1)} all-gather(bf16[256,1,128]{0,2,1:T(8,128)(2,1)S(1)} %pad_maximum_fusion), channel_id=1, replica_groups=mesh['role'=2,'seq'=4,'tp'=4] {'role','seq'}, dimensions={0}, use_global_device_ids=true | all-gather | bytes 589824 | tf_op jit(solution)/shard_map/all_gather | solution.py:105
  255.1 1.2 convolution_convert_fusion
  256.3 26.6 %all-gather = bf16[2048,128]{1,0:T(8,128)(2,1)S(1)} all-gather(bf16[256,128]{1,0:T(8,128)(2,1)S(1)} %convolution_convert_fusion), channel_id=2, replica_groups=mesh['role'=2,'seq'=4,'tp'=4] {'role','seq'}, dimensions={0}, use_global_device_ids=true | all-gather | bytes 589824 | tf_op jit(solution)/shard_map/all_gather | solution.py:106
  283.0 0.3 fusion.36
  283.3 0.4 subtract_convert_fusion
  283.7 2.8 fusion
  286.6 4.0 %fusion.1 = f32[8,256]{1,0:T(8,128)S(1)} fusion(f32[2048,256,8]{1,0,2:T(8,128)S(1)} %get-tuple-element.17, f32[8,256]{1,0:T(8,128)S(1)} %broadcast_maximum_fusion, pred[256,2048]{0,1:T(8,128)(4,1)S(1)} %iota_compare_fusion), kind=kLoop, calls=%fused_computation.7 | loop fusion | flops 20969472 | bytes 17317888 | tf_op jit(solution)/shard_map/reduce_sum | solution.py:116
  290.6 4.9 %divide_convert_fusion = bf16[8,256,128]{1,2,0:T(8,128)(2,1)} fusion(f32[2048,256,8]{1,0,2:T(8,128)S(1)} %get-tuple-element.17, f32[8,256]{1,0:T(8,128)S(1)} %broadcast_maximum_fusion, pred[256,2048]{0,1:T(8,128)(4,1)S(1)} %iota_compare_fusion, bf16[2048,128]{1,0:T(8,128)(2,1)S(1)} %all-gather, f32[8,256]{1,0:T(8,128)S(1)} %fusion.1), kind=kOutput, calls=%fused_computation.21 | convolution fusion | flops 1095237632 | bytes 18366464 | tf_op jit(solution)/shard_map/hgqk,khd->hgqd/dot_general | solution.py:117
  295.5 2.0 copy.29
  (23 shorter events, 0.1 us)
Async XLA Ops:
  7.2 28.8 %copy-start = (bf16[1280,1024]{1,0:T(8,128)(2,1)S(1)}, bf16[1280,1024]{1,0:T(8,128)(2,1)}, u32[]{:S(2)}) copy-start(bf16[1280,1024]{1,0:T(8,128)(2,1)} %param.9) | copy-start | bytes 7864324
  7.2 28.8 %all-gather.4.cloned.1.call-start = ((), (), s32[]{:S(2)}) async-start(), calls=%async_computation.4 | async-start | bytes 1474560 | tf_op jit(solution)/shard_map/all_gather | solution.py:35
  9.7 116.1 %reduce-scatter.2.cloned.1.call-start = ((), (), s32[]{:S(2)}) async-start(), calls=%async_computation.5 | async-start | bytes 2621440 | tf_op jit(solution)/shard_map/reduce_scatter | solution.py:28
  90.5 1.5 copy-start.4
  92.1 41.3 %copy-start.3 = (bf16[2048]{0:T(1024)(128)(2,1)S(1)}, bf16[2048]{0:T(1024)(128)(2,1)}, u32[]{:S(2)}) copy-start(bf16[2048]{0:T(1024)(128)(2,1)} %param.12) | copy-start | bytes 12292
  95.2 33.4 %all-to-all-start = ((s32[8,1,16]{2,1,0:T(1,128)}), s32[8,1,16]{2,1,0:T(1,128)S(1)}, u32[]{:S(2)}, u32[]{:S(2)}) async-start(s32[8,1,16]{2,1,0:T(1,128)} %bitcast), calls=%async_computation | async-start | bytes 8192 | tf_op jit(solution)/shard_map/all_to_all | solution.py:77
  128.7 19.4 %all-to-all-start.2 = ((bf16[8,16,2048]{2,1,0:T(8,128)(2,1)}), bf16[8,16,2048]{2,1,0:T(8,128)(2,1)S(1)}, u32[]{:S(2)}, u32[]{:S(2)}) async-start(bf16[8,16,2048]{2,1,0:T(8,128)(2,1)} %bitcast.4), calls=%async_computation.3 | async-start | bytes 1048576 | tf_op jit(solution)/shard_map/all_to_all | solution.py:76
  133.3 81.8 %all-gather.6.cloned.1.call-start = ((), (), s32[]{:S(2)}) async-start(), calls=%async_computation.6 | async-start | bytes 5242880 | tf_op jit(solution)/shard_map/all_gather | solution.py:87
  215.1 4.8 %copy-start.1 = (bf16[256,8192]{1,0:T(8,128)(2,1)S(1)}, bf16[256,8192]{1,0:T(8,128)(2,1)}, u32[]{:S(2)}) copy-start(bf16[256,8192]{1,0:T(8,128)(2,1)} %all-gather.6.cloned.1.call-done) | copy-start | bytes 12582916
  219.9 35.2 %copy-start.2 = (bf16[8192,128]{1,0:T(8,128)(2,1)S(1)}, bf16[8192,128]{1,0:T(8,128)(2,1)}, u32[]{:S(2)}) copy-start(bf16[8192,128]{1,0:T(8,128)(2,1)} %param.15) | copy-start | bytes 6291460
Sparse Core Ops, SparseCore 0:
  9.8 26.1 all-gather.3
  92.2 33.6 reduce-scatter.1
  164.8 50.2 all-gather.5
where the time goes:
time: 305 us; the launch traced here: 304 us
  waiting for transfers between devices  118 us (39%)
  blocking collectives  114 us (37%)
  matrix products  24.7 us (8%)
  local copies, waits for them, and re-layouts  14.7 us (5%)
  between operations  14 us (5%)
  other arithmetic  11.2 us (4%)
  starting transfers between devices  7.98 us (3%)
    all_to_all x1, blocking collectives, body(): lax.all_to_all(strips, ('role', 'seq'), split_axis=0, concat_axis=1, tile...  51.7 us
    all_gather x1, waiting for transfers between devices, body(): shard_piece = lax.all_gather(normed, 'tp', axis=1, tiled=True)  49.5 us
    reduce_scatter x1, waiting for transfers between devices, sum_hidden(): lax.psum_scatter(partial_value, 'tp', scatter_dimension=1, tiled=True)  27.3 us
    all_gather x1, blocking collectives, body(): lax.all_gather(value_rows, ('role', 'seq'), axis=0, tiled=True)  26.6 us
    all_gather x1, blocking collectives, body(): key_piece = lax.all_gather(key_rows, ('role', 'seq'), axis=0, tiled=True)  26.5 us
    all_gather x1, waiting for transfers between devices, project_strips(): lax.all_gather(merger_hidden, ('role', 'seq'), axis=0, tiled=True)  26.2 us
    all_to_all x1, waiting for transfers between devices, body(): lax.all_to_all(outgoing, ('role', 'seq'), split_axis=0, concat_axis=0, ti...  14.6 us
    dot_general x3, matrix products, body(): jnp.dot(shard_piece, table, preferred_element_type=jnp.float32)  14.2 us
  transfers between devices with their start and end apart: 5, of which 4 were waited for; matrix products, arithmetic and copies ran while one was open for 2% of the time, Pallas kernels for 0%

commit v1 on v0

--- a/solution.py
+++ b/solution.py
@@ -102,8 +102,13 @@
     value_rows = value_sum.astype(jnp.bfloat16).reshape(tok_count, local_kv, HEAD_DIM)
     score_scale = 1.0 / math.sqrt(HEAD_DIM)
     running_max = jnp.full((local_kv, group_size, tok_count), -1e30, jnp.float32)
-    key_piece = lax.all_gather(key_rows, ("role", "seq"), axis=0, tiled=True)
-    value_piece = lax.all_gather(value_rows, ("role", "seq"), axis=0, tiled=True)
+    key_piece, value_piece = jnp.split(
+        lax.all_gather(
+            jnp.concatenate([key_rows, value_rows], axis=1), ("role", "seq"), axis=0, tiled=True
+        ),
+        [key_rows.shape[1]],
+        axis=1,
+    )
     scores = (
         jnp.einsum("qhgd,khd->hgqk", queries, key_piece, preferred_element_type=jnp.float32)
         * score_scale

time: 305 us -> 269 us (0.88)
  blocking collectives: 114 us -> 60.6 us
  waiting for transfers between devices: 118 us -> 130 us
    all_gather x2 -> x0, blocking collectives: 53.1 us -> none  [the longest x1 26.6 us: body(): lax.all_gather(value_rows, ('role', 'seq'), axis=0, tiled=True)]
    all_gather x0 -> x1, waiting for transfers between devices: none -> 12.7 us  [body(): lax.all_gather(jnp.concatenate([key_rows, value_rows], axis=1), ('role',...]
  transfers between devices with their start and end apart: 5 -> 6, of which waited for: 4 -> 5; matrix products, arithmetic and copies ran while one was open for 2% -> 7% of each run, Pallas kernels for 0% -> 0%
where the time goes in v1:
time: 269 us; the launch traced here: 268 us
  waiting for transfers between devices  130 us (48%)
  blocking collectives  60.6 us (23%)
  matrix products  27.5 us (10%)
  local copies, waits for them, and re-layouts  14.7 us (5%)
  between operations  14 us (5%)
  other arithmetic  12.9 us (5%)
  starting transfers between devices  8.21 us (3%)
    all_to_all x1, blocking collectives, body(): lax.all_to_all(strips, ('role', 'seq'), split_axis=0, concat_axis=1, tile...  51.7 us
    all_gather x1, waiting for transfers between devices, body(): shard_piece = lax.all_gather(normed, 'tp', axis=1, tiled=True)  49.2 us
    reduce_scatter x1, waiting for transfers between devices, sum_hidden(): lax.psum_scatter(partial_value, 'tp', scatter_dimension=1, tiled=True)  27.3 us
    all_gather x1, waiting for transfers between devices, project_strips(): lax.all_gather(merger_hidden, ('role', 'seq'), axis=0, tiled=True)  26.2 us
    dot_general x3, matrix products, body(): jnp.dot(shard_piece, table, preferred_element_type=jnp.float32)  15.4 us
    all_to_all x1, waiting for transfers between devices, body(): lax.all_to_all(outgoing, ('role', 'seq'), split_axis=0, concat_axis=0, ti...  14.6 us
    all_gather x1, waiting for transfers between devices, body(): lax.all_gather(jnp.concatenate([key_rows, value_rows], axis=1), ('role',...  12.7 us
    psum x1, blocking collectives, body(): squares = lax.psum(jnp.sum(widened * widened, axis=1), 'tp')  8.93 us
  transfers between devices with their start and end apart: 6, of which 5 were waited for; matrix products, arithmetic and copies ran while one was open for 7% of the time, Pallas kernels for 0%

profile of v1, /device:TPU:0, one launch (start us, length us, event | category | flops | bytes accessed | tf_op | source)
XLA Modules:
  0.0 268.1 jit_solution(10362647996271629054)
XLA Ops:
  7.2 0.0 copy-start
  7.2 0.0 all-gather.4.cloned.1.call-start
  7.2 2.5 copy.46
  9.7 0.0 all-gather.4.cloned.1.call-update
  9.7 0.0 reduce-scatter.2.cloned.1.call-start
  9.8 26.2 %all-gather.4.cloned.1.call-done = bf16[512,1280]{1,0:T(8,128)(2,1)} async-done(((bf16[64,1280]{1,0:T(8,128)(2,1)}), bf16[512,1280]{1,0:T(8,128)(2,1)}) %all-gather.4.cloned.1.call-update) | async-done | bytes 1310736 | tf_op jit(solution)/shard_map/all_gather | solution.py:35
  36.0 2.8 %fusion.36 = f32[512,1024]{1,0:T(8,128)S(1)} fusion(bf16[512,1280]{1,0:T(8,128)(2,1)} %all-gather.4.cloned.1.call-done, bf16[1280,1024]{1,0:T(8,128)(2,1)S(1)} %copy-done), kind=kOutput, calls=%fused_computation.73 | convolution fusion | flops 1342177280 | bytes 6029312 | tf_op jit(solution)/shard_map/dot_general | solution.py:34
  38.8 51.7 %all_to_all.33 = f32[8,64,1024]{2,1,0:T(8,128)S(1)} all-to-all(f32[8,64,1024]{2,1,0:T(8,128)S(1)} %bitcast.68), channel_id=1, replica_groups=mesh['role'=2,'seq'=4,'tp'=4] {'role','seq'}, dimensions={0} | all-to-all | bytes 4194304 | tf_op jit(solution)/shard_map/all_to_all | solution.py:59
  90.5 1.5 copy.38
  92.0 0.0 reduce-scatter.2.cloned.1.call-update
  92.1 0.1 fusion.25
  92.2 0.1 reduce_window_sum.11
  92.3 0.2 select_reduce_fusion
  92.5 0.8 scatter_custom_fusion
  93.3 0.1 pad_add_fusion
  93.3 1.2 gather_fusion
  94.6 0.7 all_to_all.23
  95.2 3.3 %all-to-all-start = ((s32[8,1,16]{2,1,0:T(1,128)}), s32[8,1,16]{2,1,0:T(1,128)S(1)}, u32[]{:S(2)}, u32[]{:S(2)}) async-start(s32[8,1,16]{2,1,0:T(1,128)} %bitcast), calls=%async_computation | async-start | bytes 8192 | tf_op jit(solution)/shard_map/all_to_all | solution.py:77
  98.5 27.3 %reduce-scatter.2.cloned.1.call-done = f32[64,2048]{1,0:T(8,128)} async-done(((f32[64,8192]{1,0:T(8,128)}), f32[64,2048]{1,0:T(8,128)}) %reduce-scatter.2.cloned.1.call-update) | async-done | bytes 524304 | tf_op jit(solution)/shard_map/reduce_scatter | solution.py:28
  125.9 1.1 convert_element_type.54
  127.0 1.7 gather_fusion.1
  128.7 4.6 %all-to-all-start.2 = ((bf16[8,16,2048]{2,1,0:T(8,128)(2,1)}), bf16[8,16,2048]{2,1,0:T(8,128)(2,1)S(1)}, u32[]{:S(2)}, u32[]{:S(2)}) async-start(bf16[8,16,2048]{2,1,0:T(8,128)(2,1)} %bitcast.4), calls=%async_computation.3 | async-start | bytes 1048576 | tf_op jit(solution)/shard_map/all_to_all | solution.py:76
  133.3 0.0 all-gather.6.cloned.1.call-start
  133.4 0.1 select_n.56
  133.5 14.6 %all-to-all-done.2 = bf16[8,16,2048]{2,1,0:T(8,128)(2,1)S(1)} async-done(((bf16[8,16,2048]{2,1,0:T(8,128)(2,1)}), bf16[8,16,2048]{2,1,0:T(8,128)(2,1)S(1)}, u32[]{:S(2)}, u32[]{:S(2)}) %all-to-all-start.2) | async-done | bytes 524320 | tf_op jit(solution)/shard_map/all_to_all | solution.py:76
  148.0 3.7 %scatter_fusion = bf16[256,2048]{1,0:T(8,128)(2,1)} fusion(bf16[256,2048]{1,0:T(8,128)(2,1)} %copy.46, s32[128]{0:T(128)S(1)} %fusion.27, bf16[128,2048]{1,0:T(8,128)(2,1)S(1)} %bitcast.67), kind=kCustom, calls=%fused_computation.3 | custom fusion | bytes 1573376 | tf_op jit(solution)/shard_map/scatter | solution.py:81
  151.7 1.5 fusion.7
  153.2 8.9 %psum.7 = f32[256]{0:T(256)S(1)} all-reduce(f32[256]{0:T(256)S(1)} %fusion.7), channel_id=1, replica_groups=mesh['role'=2,'seq'=4,'tp'=4] {'tp'}, use_global_device_ids=true, to_apply=%region_6.7 | all-reduce | flops 256 | bytes 2048 | tf_op jit(solution)/shard_map/psum | solution.py:83
  162.2 2.5 fusion.9
  164.7 0.0 all-gather.6.cloned.1.call-update
  164.7 0.2 all-gather.8.cloned.1.call-start
  165.0 0.5 multiply_cosine_fusion
  165.5 0.3 iota_compare_fusion
  165.8 49.2 %all-gather.6.cloned.1.call-done = bf16[256,8192]{1,0:T(8,128)(2,1)} async-done(((bf16[256,2048]{1,0:T(8,128)(2,1)}), bf16[256,8192]{1,0:T(8,128)(2,1)}) %all-gather.6.cloned.1.call-update) | async-done | bytes 4194320 | tf_op jit(solution)/shard_map/all_gather | solution.py:87
  215.1 4.5 %convolution_bitcast_fusion.1 = f32[256,1,128]{0,2,1:T(8,128)S(1)} fusion(bf16[256,8192]{1,0:T(8,128)(2,1)} %all-gather.6.cloned.1.call-done, bf16[8192,128]{1,0:T(8,128)(2,1)} %param.14), kind=kOutput, calls=%fused_computation.19 | convolution fusion | flops 536870912 | bytes 6422528 | tf_op jit(solution)/shard_map/dot_general | solution.py:89
  219.6 0.3 fusion.22
  219.9 1.5 fusion.10
  221.5 0.6 pad_maximum_fusion
  222.1 0.0 all-gather.8.cloned.1.call-update
  222.1 9.4 %convolution_bitcast_fusion = f32[32,8,8,128]{3,1,2,0:T(8,128)S(1)} fusion(bf16[256,8192]{1,0:T(8,128)(2,1)} %all-gather.6.cloned.1.call-done, bf16[8192,1024]{1,0:T(8,128)(2,1)} %param.13), kind=kOutput, calls=%fused_computation.18 | convolution fusion | flops 4294967296 | bytes 22020096 | tf_op jit(solution)/shard_map/dot_general | solution.py:89
  231.6 0.2 copy.39
  231.8 0.3 fusion.35
  232.1 1.4 subtract_convert_fusion
  233.5 12.7 %all-gather.8.cloned.1.call-done = bf16[2048,2,128]{0,2,1:T(8,128)(2,1)} async-done(((bf16[256,2,128]{0,2,1:T(8,128)(2,1)}), bf16[2048,2,128]{0,2,1:T(8,128)(2,1)}) %all-gather.8.cloned.1.call-update) | async-done | bytes 1048592 | tf_op jit(solution)/shard_map/all_gather | solution.py:106
  246.2 4.2 %fusion = (f32[8,256]{1,0:T(8,128)S(1)}, f32[2048,256,8]{1,0,2:T(8,128)S(1)}) fusion(pred[256,2048]{0,1:T(8,128)(4,1)S(1)} %iota_compare_fusion, bf16[256,8,64]{2,0,1:T(8,128)(2,1)} %get-tuple-element.9, bf16[256,8,64]{2,0,1:T(8,128)(2,1)} %get-tuple-element.8, bf16[2048,2,128]{0,2,1:T(8,128)(2,1)} %all-gather.8.cloned.1.call-done), kind=kOutput, calls=%fused_computation.6 | convolution fusion | flops 1087371264 | bytes 18882560 | tf_op jit(solution)/shard_map/qhgd,khd->hgqk/dot_general | solution.py:113
  250.5 4.0 %fusion.1 = f32[8,256]{1,0:T(8,128)S(1)} fusion(f32[2048,256,8]{1,0,2:T(8,128)S(1)} %get-tuple-element.17, f32[8,256]{1,0:T(8,128)S(1)} %broadcast_maximum_fusion, pred[256,2048]{0,1:T(8,128)(4,1)S(1)} %iota_compare_fusion), kind=kLoop, calls=%fused_computation.7 | loop fusion | flops 20969472 | bytes 17317888 | tf_op jit(solution)/shard_map/reduce_sum | solution.py:121
  254.5 5.0 %divide_convert_fusion = bf16[8,256,128]{1,2,0:T(8,128)(2,1)} fusion(f32[2048,256,8]{1,0,2:T(8,128)S(1)} %get-tuple-element.17, f32[8,256]{1,0:T(8,128)S(1)} %broadcast_maximum_fusion, pred[256,2048]{0,1:T(8,128)(4,1)S(1)} %iota_compare_fusion, bf16[2048,2,128]{0,2,1:T(8,128)(2,1)S(1)} %copy-done.3, f32[8,256]{1,0:T(8,128)S(1)} %fusion.1), kind=kOutput, calls=%fused_computation.22 | convolution fusion | flops 1095237632 | bytes 18366464 | tf_op jit(solution)/shard_map/hgqk,khd->hgqd/dot_general | solution.py:122
  259.5 2.0 copy.31
  (26 shorter events, 0.1 us)
Async XLA Ops:
  7.2 28.8 %copy-start = (bf16[1280,1024]{1,0:T(8,128)(2,1)S(1)}, bf16[1280,1024]{1,0:T(8,128)(2,1)}, u32[]{:S(2)}) copy-start(bf16[1280,1024]{1,0:T(8,128)(2,1)} %param.9) | copy-start | bytes 7864324
  7.2 28.8 %all-gather.4.cloned.1.call-start = ((), (), s32[]{:S(2)}) async-start(), calls=%async_computation.4 | async-start | bytes 1474560 | tf_op jit(solution)/shard_map/all_gather | solution.py:35
  9.7 116.1 %reduce-scatter.2.cloned.1.call-start = ((), (), s32[]{:S(2)}) async-start(), calls=%async_computation.5 | async-start | bytes 2621440 | tf_op jit(solution)/shard_map/reduce_scatter | solution.py:28
  90.5 1.5 copy-start.5
  92.1 41.3 %copy-start.4 = (bf16[2048]{0:T(1024)(128)(2,1)S(1)}, bf16[2048]{0:T(1024)(128)(2,1)}, u32[]{:S(2)}) copy-start(bf16[2048]{0:T(1024)(128)(2,1)} %param.12) | copy-start | bytes 12292
  95.2 33.4 %all-to-all-start = ((s32[8,1,16]{2,1,0:T(1,128)}), s32[8,1,16]{2,1,0:T(1,128)S(1)}, u32[]{:S(2)}, u32[]{:S(2)}) async-start(s32[8,1,16]{2,1,0:T(1,128)} %bitcast), calls=%async_computation | async-start | bytes 8192 | tf_op jit(solution)/shard_map/all_to_all | solution.py:77
  128.7 19.4 %all-to-all-start.2 = ((bf16[8,16,2048]{2,1,0:T(8,128)(2,1)}), bf16[8,16,2048]{2,1,0:T(8,128)(2,1)S(1)}, u32[]{:S(2)}, u32[]{:S(2)}) async-start(bf16[8,16,2048]{2,1,0:T(8,128)(2,1)} %bitcast.4), calls=%async_computation.3 | async-start | bytes 1048576 | tf_op jit(solution)/shard_map/all_to_all | solution.py:76
  133.3 81.8 %all-gather.6.cloned.1.call-start = ((), (), s32[]{:S(2)}) async-start(), calls=%async_computation.6 | async-start | bytes 5242880 | tf_op jit(solution)/shard_map/all_gather | solution.py:87
  164.7 81.5 %all-gather.8.cloned.1.call-start = ((), (), s32[]{:S(2)}) async-start(), calls=%async_computation.7 | async-start | bytes 1179648 | tf_op jit(solution)/shard_map/all_gather | solution.py:106
  215.1 4.8 %copy-start.1 = (bf16[256,8192]{1,0:T(8,128)(2,1)S(1)}, bf16[256,8192]{1,0:T(8,128)(2,1)}, u32[]{:S(2)}) copy-start(bf16[256,8192]{1,0:T(8,128)(2,1)} %all-gather.6.cloned.1.call-done) | copy-start | bytes 12582916
  215.1 4.8 %copy-start.2 = (bf16[8192,128]{1,0:T(8,128)(2,1)S(1)}, bf16[8192,128]{1,0:T(8,128)(2,1)}, u32[]{:S(2)}) copy-start(bf16[8192,128]{1,0:T(8,128)(2,1)} %param.15) | copy-start | bytes 6291460
  250.4 4.0 %copy-start.3 = (bf16[2048,2,128]{0,2,1:T(8,128)(2,1)S(1)}, bf16[2048,2,128]{0,2,1:T(8,128)(2,1)}, u32[]{:S(2)}) copy-start(bf16[2048,2,128]{0,2,1:T(8,128)(2,1)} %all-gather.8.cloned.1.call-done) | copy-start | bytes 3145732
Sparse Core Ops, SparseCore 0:
  9.8 26.1 all-gather.3
  92.2 33.6 reduce-scatter.1
  164.8 50.2 all-gather.5
  222.3 23.8 all-gather.7
